TPU v7x, 256 devices: a whole 4x4x8 slice. The times are simulated.
256 devices in a mesh: ctx: 32 (over y, z_lo, core), tp: 8 (over x, z_hi).
Axes of the slice: x: 4, y: 4, z: 8 (z_hi: 2, z_lo: 4; z = z_hi * 4 + z_lo), core: 2. Of those that a mesh axis runs over, the one named last changes fastest.
Arguments:
- tokens: bfloat16 [12288, 3072], P('ctx', 'tp'), may hold values from -6 to 6
- queries: bfloat16 [12288, 2048], P('ctx', 'tp'), may hold values from -16 to 16
- key_rows: bfloat16 [12288, 2048], P('ctx', 'tp'), may hold values from -16 to 16
- value_rows: bfloat16 [12288, 2048], P('ctx', 'tp'), may hold values from -6 to 6
- clip_ids: int32 [12288], replicated, may hold values from 0 to 3, never falling along the last dimension, each value on 1 to 9216 neighbouring positions
- causal: int32 [4], replicated, may hold values 0 or 1
- modulation: float32 [3, 4, 3072], replicated, may hold values from -3 to 3
- w_mlp: bfloat16 [3072, 6144], P(None, 'tp'), may hold values from -0.109375 to 0.109375
- w_attn_out: bfloat16 [2048, 3072], P('tp'), may hold values from -1 to 1
- w_mlp_out: bfloat16 [6144, 3072], P('tp'), may hold values from -0.078125 to 0.078125
Outputs:
- mixed: float32 [12288, 3072], P(('ctx', 'tp'))
Inputs may be any that keep to these rules, and one draw needn't show every extreme that they name: `clip_ids`: clip numbers never fall along the tokens; each of the 4 clips has 1 to 9216 tokens and one has exactly 9216.
All inputs are finite; a program needn't handle non-finite values.
Results may differ from a plain program's by a relative error of at most 0.0065.
Values may be sent and summed in bfloat16 or wider, within the bound.
A program may use at most 128 MiB of HBM per device.

v0:
```python
import math
import jax
import jax.numpy as jnp
from jax import lax
from jax.sharding import PartitionSpec as P

HD = 128
neg_large = -1e30
eps_norm = 1e-06


def per_token(clip_rows, table):
    onehot = (clip_rows[:, None] == jnp.arange(table.shape[0], dtype=jnp.int32)[None, :]).astype(
        jnp.float32
    )
    return jnp.dot(onehot, table, precision=lax.Precision.HIGHEST)


def causal_rows(clip_rows, causal):
    matches = clip_rows[:, None] == jnp.arange(causal.shape[0], dtype=jnp.int32)[None, :]
    return jnp.sum(jnp.where(matches, causal[None, :], 0), axis=1)


def visible(query_ids, query_pos, query_causal, key_ids, key_pos):
    same_clip = query_ids[:, None] == key_ids[None, :]
    earlier = key_pos[None, :] <= query_pos[:, None]
    return same_clip & ((query_causal[:, None] == 0) | earlier)


def attend(carry_state, query_tile, allowed, key_tile, value_tile, inverse_root):
    numerator, running_max, denominator = carry_state
    scores = (
        jnp.einsum("ihd,jhd->hij", query_tile, key_tile, preferred_element_type=jnp.float32)
        * inverse_root
    )
    scores = jnp.where(allowed[None], scores, neg_large)
    new_max = jnp.maximum(running_max, jnp.transpose(jnp.max(scores, axis=2)))
    weights = jnp.where(allowed[None], jnp.exp(scores - jnp.transpose(new_max)[:, :, None]), 0.0)
    rounded = weights.astype(jnp.bfloat16)
    factor = jnp.exp(running_max - new_max)
    numerator = numerator * factor[:, :, None] + jnp.einsum(
        "hij,jhd->ihd", rounded, value_tile, preferred_element_type=jnp.float32
    )
    denominator = denominator * factor + jnp.transpose(jnp.sum(rounded.astype(jnp.float32), axis=2))
    return (numerator, new_max, denominator)


def attend_some(carry_state, query_tile, allowed, key_tile, value_tile, inverse_root):
    return attend(carry_state, query_tile, allowed, key_tile, value_tile, inverse_root)


def per_device(
    tokens,
    queries,
    key_rows,
    value_rows,
    clip_ids,
    causal,
    modulation,
    w_mlp,
    w_attn_out,
    w_mlp_out,
):
    local_rows = queries.shape[0]
    heads_local = queries.shape[1] // HD
    inverse_root = 1.0 / math.sqrt(HD)
    tp_size = lax.axis_size("tp")
    first_row = lax.axis_index("ctx") * local_rows
    own_pos = first_row + jnp.arange(local_rows, dtype=jnp.int32)
    own_ids = lax.dynamic_slice_in_dim(clip_ids, first_row, local_rows)
    own_causal = causal_rows(own_ids, causal)
    own_query = queries.reshape(local_rows, heads_local, HD)
    start_state = (
        jnp.zeros((local_rows, heads_local, HD), jnp.float32),
        jnp.full((local_rows, heads_local), neg_large, jnp.float32),
        jnp.zeros((local_rows, heads_local), jnp.float32),
    )
    whole_rows = lax.all_gather(tokens, "tp", axis=1, tiled=True)
    token_values = whole_rows.astype(jnp.float32)
    row_mean = jnp.mean(token_values, axis=1, keepdims=True)
    centred = token_values - row_mean
    row_var = jnp.mean(centred * centred, axis=1, keepdims=True)
    normed = centred * lax.rsqrt(row_var + eps_norm)
    shift_rows = per_token(own_ids, modulation[0])
    scale_rows = per_token(own_ids, modulation[1])
    modulated = (normed * (1.0 + scale_rows) + shift_rows).astype(jnp.bfloat16)
    hidden = jax.nn.gelu(
        jnp.dot(modulated, w_mlp, preferred_element_type=jnp.float32), approximate=True
    ).astype(jnp.bfloat16)
    carry_state = start_state
    key_piece = lax.all_gather(key_rows, "ctx", axis=0, tiled=True)
    value_piece = lax.all_gather(value_rows, "ctx", axis=0, tiled=True)
    piece_rows = key_piece.shape[0]
    tile_rows = piece_rows
    tile_rows = local_rows * math.gcd(piece_rows // local_rows, 4)

    def one_tile(inner_state, tile_index):
        offset = tile_index * tile_rows
        key_tile = lax.dynamic_slice_in_dim(key_piece, offset, tile_rows, 0).reshape(
            tile_rows, heads_local, HD
        )
        value_tile = lax.dynamic_slice_in_dim(value_piece, offset, tile_rows, 0).reshape(
            tile_rows, heads_local, HD
        )
        key_pos = offset + jnp.arange(tile_rows, dtype=jnp.int32)
        key_ids = lax.dynamic_slice_in_dim(clip_ids, offset, tile_rows)
        allowed = visible(own_ids, own_pos, own_causal, key_ids, key_pos)
        return (
            attend_some(inner_state, own_query, allowed, key_tile, value_tile, inverse_root),
            None,
        )

    carry_state, _ = lax.scan(
        one_tile, carry_state, jnp.arange(piece_rows // tile_rows, dtype=jnp.int32)
    )
    numerator, running_max, denominator = carry_state
    attended = (
        (numerator / denominator[:, :, None])
        .astype(jnp.bfloat16)
        .reshape(local_rows, heads_local * HD)
    )
    share_rows = local_rows // tp_size
    branch = lax.psum_scatter(
        jnp.dot(attended, w_attn_out, preferred_element_type=jnp.float32)
        + jnp.dot(hidden, w_mlp_out, preferred_element_type=jnp.float32),
        "tp",
        scatter_dimension=0,
        tiled=True,
    )
    first_share = lax.axis_index("tp") * share_rows
    residual = lax.dynamic_slice_in_dim(token_values, first_share, share_rows, 0)
    gate_rows = lax.dynamic_slice_in_dim(
        per_token(own_ids, modulation[2]), first_share, share_rows, 0
    )
    return residual + gate_rows * branch


def solution(mesh):
    in_specs = (
        P("ctx", "tp"),
        P("ctx", "tp"),
        P("ctx", "tp"),
        P("ctx", "tp"),
        P(),
        P(),
        P(),
        P(None, "tp"),
        P("tp", None),
        P("tp", None),
    )
    out_specs = P(("ctx", "tp"), None)
    return jax.shard_map(
        per_device, mesh=mesh, in_specs=in_specs, out_specs=out_specs, check_vma=False
    )
```

profile of v0, /device:TPU:1, one launch (start us, length us, event | category | flops | bytes accessed | tf_op | source)
XLA Modules:
  0.0 494.2 jit_solution(2514441145359709445)
XLA Ops:
  7.3 1.7 copy.21
  9.1 1.8 copy.23
  14.3 4.9 %fusion.19 = f32[384,3072]{1,0:T(8,128)} fusion(f32[3,4,3072]{2,1,0:T(4,128)} %param.18, s32[384]{0:T(512)S(1)} %dynamic_slice.23), kind=kOutput, calls=%fused_computation.40 | convolution fusion | flops 56624640 | bytes 4769280 | tf_op jit(solution)/shard_map/dot_general | solution.py:16
  19.3 74.0 %all-gather.4.cloned.1.call-done = bf16[384,3072]{1,0:T(8,128)(2,1)} async-done(((bf16[384,384]{1,0:T(8,128)(2,1)}), bf16[384,3072]{1,0:T(8,128)(2,1)}) %all-gather.4.cloned.1.call-update) | async-done | bytes 2359312 | tf_op jit(solution)/shard_map/all_gather | solution.py:78
  93.3 2.2 convert_reduce_fusion.1
  95.5 2.4 multiply_reduce_fusion
  98.0 6.9 %add_convert_fusion = bf16[384,3072]{1,0:T(8,128)(2,1)} fusion(f32[384,3072]{1,0:T(8,128)} %fusion.19, bf16[384,3072]{1,0:T(8,128)(2,1)S(1)} %copy-done.2, f32[384]{0:T(512)S(1)} %add_rsqrt_fusion, f32[384]{0:T(512)S(1)} %broadcast_multiply_fusion, f32[3,4,3072]{2,1,0:T(4,128)} %param.18, s32[384]{0:T(512)S(1)} %dynamic_slice.23), kind=kOutput, calls=%fused_computation.19 | convolution fusion | flops 64882176 | bytes 9490944 | tf_op jit(solution)/shard_map/dot_general | solution.py:16
  104.9 11.6 %fusion.12 = f32[384,3072]{1,0:T(8,128)} fusion(bf16[768,3072]{1,0:T(8,128)(2,1)} %param.21, bf16[384,3072]{1,0:T(8,128)(2,1)} %add_convert_fusion, bf16[3072,768]{1,0:T(8,128)(2,1)} %param.19), kind=kOutput, calls=%fused_computation.32 | convolution fusion | flops 3626532864 | bytes 16515072 | tf_op jit(solution)/shard_map/dot_general | solution.py:125
  116.5 42.9 %all-gather.6.cloned.1.call-done = bf16[12288,256]{0,1:T(8,128)(2,1)} async-done(((bf16[384,256]{0,1:T(8,128)(2,1)}), bf16[12288,256]{0,1:T(8,128)(2,1)}) %all-gather.6.cloned.1.call-update) | async-done | bytes 6291472 | tf_op jit(solution)/shard_map/all_gather | solution.py:91
  159.4 68.4 %all-gather.8.cloned.1.call-done = bf16[12288,256]{0,1:T(8,128)(2,1)} async-done(((bf16[384,256]{0,1:T(8,128)(2,1)}), bf16[12288,256]{0,1:T(8,128)(2,1)}) %all-gather.8.cloned.1.call-update) | async-done | bytes 6291472 | tf_op jit(solution)/shard_map/all_gather | solution.py:92
  228.3 118.4 %while.15 = (s32[]{:T(128)}, f32[384,2,128]{0,2,1:T(8,128)S(1)}, f32[384,2]{0,1:T(2,128)S(1)}, f32[384,2]{0,1:T(2,128)S(1)}, s32[384]{0:T(512)S(1)}, /*index=5*/...) while((s32[]{:T(128)}, f32[384,2,128]{0,2,1:T(8,128)S(1)}, ...), condition=%wide.region_4.5_spmd.clone, body=%wide.region_1.4_spmd.clone.sunk | while | flops 624334848 | bytes 41178116 | solution.py:113
  234.3 3.3 fusion.51
  237.6 3.7 convert_reduce_fusion.3
  249.1 3.3 fusion.51
  252.4 3.7 convert_reduce_fusion.3
  263.9 3.3 fusion.51
  267.2 3.7 convert_reduce_fusion.3
  278.7 3.3 fusion.51
  282.0 3.7 convert_reduce_fusion.3
  293.5 3.3 fusion.51
  296.8 3.7 convert_reduce_fusion.3
  308.3 3.3 fusion.51
  311.6 3.7 convert_reduce_fusion.3
  323.1 3.3 fusion.51
  326.4 3.7 convert_reduce_fusion.3
  337.9 3.3 fusion.51
  341.2 3.7 convert_reduce_fusion.3
  346.7 5.3 %convolution_add_fusion = f32[384,3072]{1,0:T(8,128)} fusion(f32[384,3072]{1,0:T(8,128)} %fusion.12, bf16[384,256]{0,1:T(8,128)(2,1)S(1)} %bitcast.71, bf16[256,3072]{1,0:T(8,128)(2,1)S(1)} %copy-done), kind=kOutput, calls=%fused_computation.21 | convolution fusion | flops 605159424 | bytes 11206656 | tf_op jit(solution)/shard_map/dot_general | solution.py:124
  352.0 5.1 %fusion.21 = f32[384,3072]{1,0:T(8,128)} fusion(f32[3,4,3072]{2,1,0:T(4,128)} %param.18, s32[384]{0:T(512)S(1)} %get-tuple-element.315), kind=kOutput, calls=%fused_computation.42 | convolution fusion | flops 56624640 | bytes 4769280 | tf_op jit(solution)/shard_map/dot_general | solution.py:16
  357.1 2.7 convert_element_type.21
  359.9 125.5 %reduce-scatter.2.cloned.1.call-done = f32[48,3072]{1,0:T(8,128)} async-done(((f32[384,3072]{1,0:T(8,128)}), f32[48,3072]{1,0:T(8,128)}) %reduce-scatter.2.cloned.1.call-update) | async-done | bytes 589840 | tf_op jit(solution)/shard_map/reduce_scatter | solution.py:123
  485.4 2.3 multiply_add_fusion
  (129 shorter events, 61.2 us)
Async XLA Ops:
  6.5 340.2 %copy-start = (bf16[256,3072]{1,0:T(8,128)(2,1)S(1)}, bf16[256,3072]{1,0:T(8,128)(2,1)}, u32[]{:S(2)}) copy-start(bf16[256,3072]{1,0:T(8,128)(2,1)} %param.20) | copy-start | bytes 4718596
  6.5 86.8 %all-gather.4.cloned.1.call-start = ((), (), s32[]{:S(2)}) async-start(), calls=%async_computation.1 | async-start | bytes 2654208 | tf_op jit(solution)/shard_map/all_gather | solution.py:78
  7.3 152.1 %all-gather.6.cloned.1.call-start = ((), (), s32[]{:S(2)}) async-start(), calls=%async_computation.2 | async-start | bytes 6488064 | tf_op jit(solution)/shard_map/all_gather | solution.py:91
  9.1 218.7 %all-gather.8.cloned.1.call-start = ((), (), s32[]{:S(2)}) async-start(), calls=%async_computation.3 | async-start | bytes 6488064 | tf_op jit(solution)/shard_map/all_gather | solution.py:92
  10.9 474.5 %reduce-scatter.2.cloned.1.call-start = ((), (), s32[]{:S(2)}) async-start(), calls=%async_computation.4 | async-start | bytes 5308416 | tf_op jit(solution)/shard_map/reduce_scatter | solution.py:123
  93.3 4.6 copy-start.2
  237.6 3.8 copy-start.1
  252.4 3.8 copy-start.1
  267.2 3.8 copy-start.1
  282.0 3.8 copy-start.1
  296.8 3.8 copy-start.1
  311.6 3.8 copy-start.1
  326.4 3.8 copy-start.1
  341.2 3.8 copy-start.1
  352.0 5.1 %copy-start.3 = (bf16[384,3072]{1,0:T(8,128)(2,1)S(1)}, bf16[384,3072]{1,0:T(8,128)(2,1)}, u32[]{:S(2)}) copy-start(bf16[384,3072]{1,0:T(8,128)(2,1)} %all-gather.4.cloned.1.call-done) | copy-start | bytes 7077892
Sparse Core Ops, SparseCore 0:
  9.8 83.4 all-gather.3
  95.1 64.1 all-gather.5
  161.2 66.5 all-gather.7
  352.1 133.2 reduce-scatter.1
where the time goes:
time: 496 us; the launch traced here: 494 us
  waiting for transfers between devices  312 us (63%)
  matrix products  73.8 us (15%)
  other arithmetic  55.2 us (11%)
  local copies, waits for them, and re-layouts  34.7 us (7%)
  between operations  13.2 us (3%)
  loops' own time  5.58 us (1%)
    reduce_scatter x1, waiting for transfers between devices, per_device(): lax.psum_scatter(jnp.dot(attended, w_attn_out, preferred_element_type=jnp...  126 us
    all_gather x1, waiting for transfers between devices, per_device(): whole_rows = lax.all_gather(tokens, 'tp', axis=1, tiled=True)  74 us
    all_gather x1, waiting for transfers between devices, per_device(): value_piece = lax.all_gather(value_rows, 'ctx', axis=0, tiled=True)  68.4 us
    all_gather x1, waiting for transfers between devices, per_device(): key_piece = lax.all_gather(key_rows, 'ctx', axis=0, tiled=True)  42.9 us
    reduce_sum x8, other arithmetic, attend(): jnp.sum(rounded.astype(jnp.float32), axis=2)  29.8 us
    dot_general x8, matrix products, attend(): jnp.einsum('ihd,jhd->hij', query_tile, key_tile, preferred_element_type=j...  26.6 us
    dot_general x3, matrix products, per_token(): return jnp.dot(onehot, table, precision=lax.Precision.HIGHEST)  17 us
    dot_general x8, matrix products, attend(): jnp.einsum('hij,jhd->ihd', rounded, value_tile, preferred_element_type=jn...  13.4 us
  transfers between devices with their start and end apart: 4, of which 4 were waited for; matrix products, arithmetic and copies ran while one was open for 9% of the time, Pallas kernels for 0%

commit v1 on v0

--- a/solution.py
+++ b/solution.py
@@ -88,7 +88,9 @@
         jnp.dot(modulated, w_mlp, preferred_element_type=jnp.float32), approximate=True
     ).astype(jnp.bfloat16)
     carry_state = start_state
-    key_piece = lax.all_gather(key_rows, "ctx", axis=0, tiled=True)
+    key_piece = jnp.concatenate(
+        lax.all_to_all(jnp.stack([key_rows] * lax.axis_size("ctx")), "ctx", 0, 0), axis=0
+    )
     value_piece = lax.all_gather(value_rows, "ctx", axis=0, tiled=True)
     piece_rows = key_piece.shape[0]
     tile_rows = piece_rows

time: 496 us -> 526 us (1.060)
  local copies, waits for them, and re-layouts: 34.7 us -> 69.7 us
  waiting for transfers between devices: 312 us -> 298 us
  starting transfers between devices: 0.13 us -> 10.5 us
    all_to_all x0 -> x1, waiting for transfers between devices: none -> 89.9 us  [per_device(): lax.all_to_all(jnp.stack([key_rows] * lax.axis_size('ctx')), 'ctx', 0, 0)]
    all_gather x1, waiting for transfers between devices: 68.4 us -> 0.01 us  [per_device(): value_piece = lax.all_gather(value_rows, 'ctx', axis=0, tiled=True)]
    all_gather x1 -> x0, waiting for transfers between devices: 42.9 us -> none  [per_device(): key_piece = lax.all_gather(key_rows, 'ctx', axis=0, tiled=True)]
    dynamic_slice x0 -> x16, local copies, waits for them, and re-layouts: none -> 28.1 us  [one_tile(): lax.dynamic_slice_in_dim(key_piece, offset, tile_rows, 0)]
    all_to_all x0 -> x1, starting transfers between devices: none -> 10.4 us  [per_device(): lax.all_to_all(jnp.stack([key_rows] * lax.axis_size('ctx')), 'ctx', 0, 0)]
    all_to_all x0 -> x1, local copies, waits for them, and re-layouts: none -> 8.61 us  [per_device(): lax.all_to_all(jnp.stack([key_rows] * lax.axis_size('ctx')), 'ctx', 0, 0)]
    all_gather x1, waiting for transfers between devices: 74 us -> 82.4 us  [per_device(): whole_rows = lax.all_gather(tokens, 'tp', axis=1, tiled=True)]
  transfers between devices with their start and end apart: 4 -> 4, of which waited for: 4 -> 3; matrix products, arithmetic and copies ran while one was open for 9% -> 10% of each run, Pallas kernels for 0% -> 0%
where the time goes in v1:
time: 526 us; the launch traced here: 523 us
  waiting for transfers between devices  298 us (57%)
  matrix products  72.6 us (14%)
  local copies, waits for them, and re-layouts  69.7 us (13%)
  other arithmetic  54.2 us (10%)
  between operations  13.2 us (3%)
  starting transfers between devices  10.5 us (2%)
    reduce_scatter x1, waiting for transfers between devices, per_device(): lax.psum_scatter(jnp.dot(attended, w_attn_out, preferred_element_type=jnp...  125 us
    all_to_all x1, waiting for transfers between devices, per_device(): lax.all_to_all(jnp.stack([key_rows] * lax.axis_size('ctx')), 'ctx', 0, 0)  89.9 us
    all_gather x1, waiting for transfers between devices, per_device(): whole_rows = lax.all_gather(tokens, 'tp', axis=1, tiled=True)  82.4 us
    reduce_sum x8, other arithmetic, attend(): jnp.sum(rounded.astype(jnp.float32), axis=2)  29.8 us
    dynamic_slice x16, local copies, waits for them, and re-layouts, one_tile(): lax.dynamic_slice_in_dim(key_piece, offset, tile_rows, 0)  28.1 us
    dot_general x8, matrix products, attend(): jnp.einsum('ihd,jhd->hij', query_tile, key_tile, preferred_element_type=j...  26.1 us
    dot_general x3, matrix products, per_token(): return jnp.dot(onehot, table, precision=lax.Precision.HIGHEST)  16.2 us
    dot_general x8, matrix products, attend(): jnp.einsum('hij,jhd->ihd', rounded, value_tile, preferred_element_type=jn...  13.4 us
  transfers between devices with their start and end apart: 4, of which 3 were waited for; matrix products, arithmetic and copies ran while one was open for 10% of the time, Pallas kernels for 0%

profile of v1, /device:TPU:1, one launch (start us, length us, event | category | flops | bytes accessed | tf_op | source)
XLA Modules:
  0.0 523.5 jit_solution(7752779272402966335)
XLA Ops:
  8.4 3.6 stack.2
  12.0 10.4 %all-to-all-start = ((bf16[32,384,256]{1,2,0:T(8,128)(2,1)}), bf16[32,384,256]{1,2,0:T(8,128)(2,1)}, u32[]{:S(2)}, u32[]{:S(2)}) async-start(bf16[32,384,256]{1,2,0:T(8,128)(2,1)} %stack.2), calls=%async_computation | async-start | bytes 12582912 | tf_op jit(solution)/shard_map/all_to_all | solution.py:92
  25.1 4.2 fusion.19
  29.3 82.4 %all-gather.3.cloned.1.call-done = bf16[384,3072]{1,0:T(8,128)(2,1)} async-done(((bf16[384,384]{1,0:T(8,128)(2,1)}), bf16[384,3072]{1,0:T(8,128)(2,1)}) %all-gather.3.cloned.1.call-update) | async-done | bytes 2359312 | tf_op jit(solution)/shard_map/all_gather | solution.py:78
  111.7 2.2 convert_reduce_fusion.1
  113.9 2.4 multiply_reduce_fusion
  116.3 6.8 %add_convert_fusion = bf16[384,3072]{1,0:T(8,128)(2,1)} fusion(f32[384,3072]{1,0:T(8,128)} %fusion.19, bf16[384,3072]{1,0:T(8,128)(2,1)S(1)} %copy-done.2, f32[384]{0:T(512)S(1)} %add_rsqrt_fusion, f32[384]{0:T(512)S(1)} %broadcast_multiply_fusion, f32[3,4,3072]{2,1,0:T(4,128)S(1)} %copy-done.6, s32[384]{0:T(512)S(1)} %dynamic_slice.23), kind=kOutput, calls=%fused_computation.19 | convolution fusion | flops 64882176 | bytes 9492480 | tf_op jit(solution)/shard_map/dot_general | solution.py:16
  123.2 11.6 %fusion.12 = f32[384,3072]{1,0:T(8,128)} fusion(bf16[768,3072]{1,0:T(8,128)(2,1)} %param.21, bf16[384,3072]{1,0:T(8,128)(2,1)} %add_convert_fusion, bf16[3072,768]{1,0:T(8,128)(2,1)} %param.19), kind=kOutput, calls=%fused_computation.32 | convolution fusion | flops 3626532864 | bytes 16515072 | tf_op jit(solution)/shard_map/dot_general | solution.py:127
  134.8 89.9 %all-to-all-done = bf16[32,384,256]{1,2,0:T(8,128)(2,1)} async-done(((bf16[32,384,256]{1,2,0:T(8,128)(2,1)}), bf16[32,384,256]{1,2,0:T(8,128)(2,1)}, u32[]{:S(2)}, u32[]{:S(2)}) %all-to-all-start) | async-done | bytes 6291488 | tf_op jit(solution)/shard_map/all_to_all | solution.py:92
  224.7 8.6 %copy.36 = bf16[32,384,256]{2,1,0:T(8,128)(2,1)} copy(bf16[32,384,256]{1,2,0:T(8,128)(2,1)} %all-to-all-done) | data formatting | bytes 12582912 | tf_op jit(solution)/shard_map/all_to_all | solution.py:92
  233.8 142.3 %while.15 = (s32[]{:T(128)}, f32[384,2,128]{0,2,1:T(8,128)S(1)}, f32[384,2]{0,1:T(2,128)S(1)}, f32[384,2]{0,1:T(2,128)S(1)}, s32[384]{0:T(512)S(1)}, /*index=5*/...) while((s32[]{:T(128)}, f32[384,2,128]{0,2,1:T(8,128)S(1)}, ...), condition=%wide.region_4.5_spmd.clone, body=%wide.region_1.4_spmd.clone.sunk | while | flops 624334848 | bytes 42750984 | solution.py:115
  241.7 3.3 fusion.51
  244.9 3.7 convert_reduce_fusion.3
  259.4 3.3 fusion.51
  262.7 3.7 convert_reduce_fusion.3
  277.2 3.3 fusion.51
  280.5 3.7 convert_reduce_fusion.3
  295.0 3.3 fusion.51
  298.3 3.7 convert_reduce_fusion.3
  312.8 3.3 fusion.51
  316.1 3.7 convert_reduce_fusion.3
  330.6 3.3 fusion.51
  333.9 3.7 convert_reduce_fusion.3
  348.4 3.3 fusion.51
  351.7 3.7 convert_reduce_fusion.3
  366.2 3.3 fusion.51
  369.5 3.7 convert_reduce_fusion.3
  376.2 5.3 %convolution_add_fusion = f32[384,3072]{1,0:T(8,128)} fusion(f32[384,3072]{1,0:T(8,128)} %fusion.12, bf16[384,256]{0,1:T(8,128)(2,1)S(1)} %bitcast.73, bf16[256,3072]{1,0:T(8,128)(2,1)S(1)} %copy-done), kind=kOutput, calls=%fused_computation.21 | convolution fusion | flops 605159424 | bytes 11206656 | tf_op jit(solution)/shard_map/dot_general | solution.py:126
  381.5 5.1 fusion.21
  386.7 2.7 convert_element_type.21
  389.4 125.2 %reduce-scatter.2.cloned.1.call-done = f32[48,3072]{1,0:T(8,128)} async-done(((f32[384,3072]{1,0:T(8,128)}), f32[48,3072]{1,0:T(8,128)}) %reduce-scatter.2.cloned.1.call-update) | async-done | bytes 589840 | tf_op jit(solution)/shard_map/reduce_scatter | solution.py:125
  514.6 2.3 multiply_add_fusion
  (154 shorter events, 86.4 us)
Async XLA Ops:
  6.5 369.6 %copy-start = (bf16[256,3072]{1,0:T(8,128)(2,1)S(1)}, bf16[256,3072]{1,0:T(8,128)(2,1)}, u32[]{:S(2)}) copy-start(bf16[256,3072]{1,0:T(8,128)(2,1)} %param.20) | copy-start | bytes 4718596
  6.5 105.2 %all-gather.3.cloned.1.call-start = ((), (), s32[]{:S(2)}) async-start(), calls=%async_computation.2 | async-start | bytes 2654208 | tf_op jit(solution)/shard_map/all_gather | solution.py:78
  12.0 10.5 %copy-start.4 = (bf16[384,256]{1,0:T(8,128)(2,1)S(1)}, bf16[384,256]{1,0:T(8,128)(2,1)}, u32[]{:S(2)}) copy-start(bf16[384,256]{1,0:T(8,128)(2,1)} %param.15) | copy-start | bytes 589828
  12.0 11.4 %copy-start.5 = (bf16[384,256]{1,0:T(8,128)(2,1)S(1)}, bf16[384,256]{1,0:T(8,128)(2,1)}, u32[]{:S(2)}) copy-start(bf16[384,256]{1,0:T(8,128)(2,1)} %param.13) | copy-start | bytes 589828
  12.0 12.5 %copy-start.7 = (s32[4]{0:T(128)S(1)}, s32[4]{0:T(128)}, u32[]{:S(2)}) copy-start(s32[4]{0:T(128)} %param.17) | copy-start | bytes 52
  12.0 13.1 %copy-start.6 = (f32[3,4,3072]{2,1,0:T(4,128)S(1)}, f32[3,4,3072]{2,1,0:T(4,128)}, u32[]{:S(2)}) copy-start(f32[3,4,3072]{2,1,0:T(4,128)} %param.18) | copy-start | bytes 442372
  12.0 212.7 %all-to-all-start = ((bf16[32,384,256]{1,2,0:T(8,128)(2,1)}), bf16[32,384,256]{1,2,0:T(8,128)(2,1)}, u32[]{:S(2)}, u32[]{:S(2)}) async-start(bf16[32,384,256]{1,2,0:T(8,128)(2,1)} %stack.2), calls=%async_computation | async-start | bytes 12582912 | tf_op jit(solution)/shard_map/all_to_all | solution.py:92
  22.4 210.9 %all-gather.5.cloned.1.call-start = ((), (), s32[]{:S(2)}) async-start(), calls=%async_computation.3 | async-start | bytes 6488064 | tf_op jit(solution)/shard_map/all_gather | solution.py:94
  23.3 491.4 %reduce-scatter.2.cloned.1.call-start = ((), (), s32[]{:S(2)}) async-start(), calls=%async_computation.4 | async-start | bytes 5308416 | tf_op jit(solution)/shard_map/reduce_scatter | solution.py:125
  111.7 4.6 copy-start.2
  244.9 5.0 copy-start.1
  262.7 5.0 copy-start.1
  280.5 5.0 copy-start.1
  298.3 5.0 copy-start.1
  316.1 5.0 copy-start.1
  333.9 5.0 copy-start.1
  351.7 5.0 copy-start.1
  369.5 5.0 copy-start.1
  381.5 5.1 copy-start.3
Sparse Core Ops, SparseCore 0:
  9.8 101.8 all-gather.2
  113.5 104.5 all-gather.4
  381.6 132.9 reduce-scatter.1
